TPU v7x, 32 devices: a whole 2x2x4 slice. The times are simulated.
32 devices in a mesh: grp: 4 (over x, core), wide: 8 (over z, y).
Axes of the slice: x: 2, y: 2, z: 4, core: 2. Of those that a mesh axis runs over, the one named last changes fastest.
Arguments:
- expression: float32 [1024, 4096], P(('grp', 'wide'))
- assignment: int32 [16], replicated, may hold values from 0 to 15, each once
- pairing: int32 [2, 16], replicated, may hold values from 0 to 15, as said below
Outputs:
- cross_scores: float32 [2, 16, 256, 256], P(None, 'wide', 'grp')
Inputs may be any that keep to these rules, and one draw needn't show every extreme that they name: Row r of pairing is round r of one round-robin plan over the 16 panels: every panel has a partner other than itself, and the partner's partner is the panel.
All inputs are finite; a program needn't handle non-finite values.
Results may differ from a plain program's by a relative error of at most 0.0043.
Values may be sent and summed in bfloat16 or wider, within the bound.
No kernel may reach another device: no remote copies, remote signals or barrier semaphores. Data moves between devices by JAX's collectives and lax.ppermute only.
A program may use at most 192 MiB of HBM per device.

v0:
```python
import jax
import jax.numpy as jnp
from jax import lax
from jax.sharding import PartitionSpec as P

PANEL = 256


def cross_terms(received):
    count = received.shape[1]
    cells = received.shape[2]
    width = received.shape[3]
    blocks = received.reshape(count, cells, width // received_panel_width(), received_panel_width())
    own = blocks[:, :, 0]
    partners = blocks[:, :, 1:]
    return jnp.einsum("mca,mcrb->rmab", own, partners, preferred_element_type=jnp.float32)


def received_panel_width():
    return PANEL


def shards(expression, assignment, pairing):
    n_wide = lax.axis_size("wide")
    n_grp = lax.axis_size("grp")
    cells = expression.shape[0]
    pan_dev = assignment.shape[0] // n_wide
    panel = expression.shape[1] // assignment.shape[0]
    rounds = pairing.shape[0]
    total = cells * n_wide * n_grp
    own_ids = assignment.reshape(n_wide, pan_dev, 1)
    partner_ids = pairing[:, assignment].T.reshape(n_wide, pan_dev, rounds)
    panel_ids = jnp.concatenate([own_ids, partner_ids], axis=2)
    columns = (panel_ids[..., None] * panel + jnp.arange(panel, dtype=jnp.int32)).reshape(-1)
    span = (1 + rounds) * panel
    picked = (
        jnp.take(expression, columns, axis=1)
        .reshape(cells, n_wide, pan_dev, span)
        .transpose(1, 2, 0, 3)
    )
    received = lax.all_to_all(picked, "wide", split_axis=0, concat_axis=2, tiled=True)
    sums = lax.psum(
        (
            jnp.sum(received, axis=2, keepdims=True),
            jnp.sum(received * received, axis=2, keepdims=True),
        ),
        "grp",
    )
    mean = sums[0] / total
    var = sums[1] / total - mean * mean
    scaled = ((received - mean) * lax.rsqrt(var + 1e-05)).astype(jnp.bfloat16)
    partial_tiles = cross_terms(scaled)
    rows_dev = panel // n_grp
    summed = lax.psum(partial_tiles, "grp")
    mine = lax.dynamic_slice_in_dim(summed, lax.axis_index("grp") * rows_dev, rows_dev, 2)
    return mine * total ** (-0.5)


def solution(mesh):
    placed = (P(("grp", "wide"), None), P(), P())
    return jax.shard_map(
        shards, mesh=mesh, in_specs=placed, out_specs=P(None, "wide", "grp", None), check_vma=False
    )
```

profile of v0, /device:TPU:0, one launch (start us, length us, event | category | flops | bytes accessed | tf_op | source)
XLA Modules:
  0.0 160.9 jit_solution(13995582573003539010)
XLA Ops:
  6.5 0.0 all-reduce.3.cloned.1.call-start
  6.5 0.7 compare_select_fusion.2
  7.2 0.7 concatenate.11
  7.9 0.1 copy.34
  8.0 0.8 copy.32
  8.8 0.6 gather_fusion
  9.3 0.1 copy.35
  9.4 0.1 copy.36
  9.5 0.1 iota_add_fusion
  9.6 0.1 add.77
  9.7 0.1 reshape.107
  9.8 0.1 compare_select_fusion
  9.9 1.6 %copy.39 = f32[32,4096]{0,1:T(8,128)S(1)} copy(f32[32,4096]{1,0:T(8,128)} %param.3) | data formatting | bytes 1048576 | tf_op args[0]
  11.6 41.0 %gather_fusion.1 = f32[12288,32]{1,0:T(8,128)} fusion(f32[32,4096]{0,1:T(8,128)S(1)} %copy.39, s32[12288]{0:T(1024)S(1)} %broadcast_clamp_fusion), kind=kCustom, calls=%fused_computation.1 | custom fusion | bytes 3194880 | tf_op jit(solution)/shard_map/jit(_take)/gather | solution.py:37
  52.6 4.4 %copy.40 = f32[32,8,2,768]{3,0,2,1:T(8,128)S(1)} copy(f32[32,8,2,768]{0,3,2,1:T(8,128)} %bitcast.26) | data formatting | bytes 3145728 | tf_op jit(solution)/shard_map/jit(_take)/gather | solution.py:37
  56.9 0.2 select_bitcast_fusion
  57.1 44.1 %all_to_all.18 = f32[8,2,32,768]{3,2,1,0:T(8,128)S(1)} all-to-all(f32[8,2,32,768]{3,2,1,0:T(8,128)S(1)} %select_bitcast_fusion), channel_id=1, replica_groups=mesh['grp'=4,'wide'=8] {'wide'}, dimensions={0} | all-to-all | bytes 3145728 | tf_op jit(solution)/shard_map/all_to_all | solution.py:41
  101.2 0.1 copy.41
  101.4 1.9 %all_to_all.16 = f32[2,256,3,256]{3,2,1,0:T(4,128)} reshape(f32[1,2,8,32,768]{4,3,2,1,0:T(8,128)S(1)} %copy.41) | data formatting | bytes 3145728 | tf_op jit(solution)/shard_map/all_to_all | solution.py:41
  103.3 0.2 bitcast_reduce_fusion
  103.4 10.1 %all-reduce = (f32[1,2,1,768]{3,1,2,0:T(2,128)S(1)}, f32[1,2,1,768]{3,1,2,0:T(2,128)S(1)}) all-reduce(f32[1,2,1,768]{3,1,2,0:T(2,128)S(1)} %bitcast.29, f32[1,2,1,768]{3,1,2,0:T(2,128)S(1)} %bitcast.28), channel_id=1, replica_groups=mesh['grp'=4,'wide'=8] {'grp'}, use_global_device_ids=true, to_apply=%region_3.4 | all-reduce | flops 3072 | bytes 24576 | tf_op jit(solution)/shard_map/psum | solution.py:42
  113.6 1.9 %fusion.1 = bf16[2,256,3,256]{3,1,0,2:T(8,128)(2,1)S(1)} fusion(f32[2,256,3,256]{3,2,1,0:T(4,128)} %all_to_all.16, f32[2,3,256]{2,0,1:T(2,128)S(1)} %bitcast.31, f32[2,3,256]{2,0,1:T(2,128)S(1)} %bitcast.30), kind=kLoop, calls=%fused_computation.4 | loop fusion | flops 1179648 | bytes 2371584 | tf_op jit(solution)/shard_map/convert_element_type | solution.py:51
  115.5 1.4 convolution_bitcast_fusion
  116.9 0.0 all-reduce.3.cloned.1.call-update
  116.9 35.5 %all-reduce.3.cloned.1.call-done = f32[2,2,256,256]{3,2,1,0:T(8,128)} async-done(((f32[2,2,256,256]{3,2,1,0:T(8,128)}), f32[2,2,256,256]{3,2,1,0:T(8,128)}) %all-reduce.3.cloned.1.call-update) | async-done | bytes 1048592 | tf_op jit(solution)/shard_map/psum | solution.py:54
  152.4 1.7 %dynamic-slice_multiply_fusion = f32[2,2,64,256]{3,2,1,0:T(8,128)} fusion(f32[2,2,256,256]{3,2,1,0:T(8,128)} %all-reduce.3.cloned.1.call-done, s32[]{:T(128)S(6)} %select_n.32), kind=kLoop, calls=%fused_computation.10 | loop fusion | flops 65536 | bytes 524292 | tf_op jit(solution)/shard_map/mul | solution.py:56
  (6 shorter events, 0.1 us)
Async XLA Ops:
  6.5 145.9 %all-reduce.3.cloned.1.call-start = ((), (), s32[]{:S(2)}) async-start(), calls=%async_computation.1 | async-start | bytes 2097152 | tf_op jit(solution)/shard_map/psum | solution.py:54
Sparse Core Ops, SparseCore 0:
  117.0 35.3 all-reduce.2
where the time goes:
time: 161 us
  blocking collectives  54.2 us (34%)
  local copies, waits for them, and re-layouts  51.5 us (32%)
  waiting for transfers between devices  35.5 us (22%)
  between operations  13.5 us (8%)
  other arithmetic  4.75 us (3%)
    gather x2, local copies, waits for them, and re-layouts, shards(): jnp.take(expression, columns, axis=1).reshape(cells, n_wide, pan_dev, span)  45.4 us
    all_to_all x1, blocking collectives, shards(): lax.all_to_all(picked, 'wide', split_axis=0, concat_axis=2, tiled=True)  44.1 us
    psum x1, waiting for transfers between devices, shards(): summed = lax.psum(partial_tiles, 'grp')  35.5 us
    psum x1, blocking collectives, shards(): lax.psum((jnp.sum(received, axis=2, keepdims=True), jnp.sum(received * re...  10.1 us
  transfers between devices with their start and end apart: 1, of which 1 were waited for; matrix products, arithmetic and copies ran while one was open for 0% of the time, Pallas kernels for 0%

commit v1 on v0

--- a/solution.py
+++ b/solution.py
@@ -51,7 +51,9 @@
     scaled = ((received - mean) * lax.rsqrt(var + 1e-05)).astype(jnp.bfloat16)
     partial_tiles = cross_terms(scaled)
     rows_dev = panel // n_grp
-    summed = lax.psum(partial_tiles, "grp")
+    summed = partial_tiles
+    for hop in (1, 2):
+        summed = summed + lax.ppermute(summed, "grp", [(dev, dev ^ hop) for dev in range(4)])
     mine = lax.dynamic_slice_in_dim(summed, lax.axis_index("grp") * rows_dev, rows_dev, 2)
     return mine * total ** (-0.5)
 

time: 161 us -> 139 us (0.86)
  between operations: 13.5 us -> 0.14 us
  waiting for transfers between devices: 35.5 us -> 26.3 us
  other arithmetic: 4.75 us -> 1.84 us
  local copies, waits for them, and re-layouts: 51.5 us -> 54.1 us
  starting transfers between devices: 0.01 us -> 1.68 us
    psum x1 -> x0, waiting for transfers between devices: 35.5 us -> none  [shards(): summed = lax.psum(partial_tiles, 'grp')]
    ppermute x0 -> x2, waiting for transfers between devices: none -> 26.3 us  [shards(): lax.ppermute(summed, 'grp', [(dev, dev ^ hop) for dev in range(4)])]
    all_to_all x2 -> x3, local copies, waits for them, and re-layouts: 2.04 us -> 3.87 us  [shards(): lax.all_to_all(picked, 'wide', split_axis=0, concat_axis=2, tiled=True)]
    ppermute x0 -> x2, starting transfers between devices: none -> 1.68 us  [shards(): lax.ppermute(summed, 'grp', [(dev, dev ^ hop) for dev in range(4)])]
    mul x1, other arithmetic: 1.67 us -> 0.04 us  [shards(): return mine * total ** (-0.5)]
  transfers between devices with their start and end apart: 1 -> 2, of which waited for: 1 -> 2; matrix products, arithmetic and copies ran while one was open for 0% -> 0% of each run, Pallas kernels for 0% -> 0%
where the time goes in v1:
time: 139 us
  blocking collectives  54.2 us (39%)
  local copies, waits for them, and re-layouts  54.1 us (39%)
  waiting for transfers between devices  26.3 us (19%)
  other arithmetic  1.84 us (1%)
  starting transfers between devices  1.68 us (1%)
    gather x2, local copies, waits for them, and re-layouts, shards(): jnp.take(expression, columns, axis=1).reshape(cells, n_wide, pan_dev, span)  45.4 us
    all_to_all x1, blocking collectives, shards(): lax.all_to_all(picked, 'wide', split_axis=0, concat_axis=2, tiled=True)  44.1 us
    ppermute x2, waiting for transfers between devices, shards(): lax.ppermute(summed, 'grp', [(dev, dev ^ hop) for dev in range(4)])  26.3 us
    psum x1, blocking collectives, shards(): lax.psum((jnp.sum(received, axis=2, keepdims=True), jnp.sum(received * re...  10.1 us
    all_to_all x3, local copies, waits for them, and re-layouts, shards(): lax.all_to_all(picked, 'wide', split_axis=0, concat_axis=2, tiled=True)  3.87 us
  transfers between devices with their start and end apart: 2, of which 2 were waited for; matrix products, arithmetic and copies ran while one was open for 0% of the time, Pallas kernels for 0%

profile of v1, /device:TPU:0, one launch (start us, length us, event | category | flops | bytes accessed | tf_op | source)
XLA Modules:
  0.0 138.6 jit_solution(7036565224072885322)
XLA Ops:
  0.0 0.7 compare_select_fusion.2
  0.7 0.7 concatenate.11
  1.4 0.1 copy.21
  1.5 0.8 copy.19
  2.2 0.6 gather_fusion
  2.8 0.1 copy.22
  2.9 0.1 copy.23
  3.0 0.1 iota_add_fusion
  3.1 0.1 add.81
  3.2 0.1 reshape.107
  3.3 0.1 compare_select_fusion
  3.4 1.6 %copy.26 = f32[32,4096]{0,1:T(8,128)S(1)} copy(f32[32,4096]{1,0:T(8,128)} %param.3) | data formatting | bytes 1048576 | tf_op args[0]
  5.0 41.0 %gather_fusion.1 = f32[12288,32]{1,0:T(8,128)} fusion(f32[32,4096]{0,1:T(8,128)S(1)} %copy.26, s32[12288]{0:T(1024)S(1)} %broadcast_clamp_fusion), kind=kCustom, calls=%fused_computation.1 | custom fusion | bytes 3194880 | tf_op jit(solution)/shard_map/jit(_take)/gather | solution.py:37
  46.0 4.4 %copy.27 = f32[32,8,2,768]{3,0,2,1:T(8,128)S(1)} copy(f32[32,8,2,768]{0,3,2,1:T(8,128)} %bitcast.27) | data formatting | bytes 3145728 | tf_op jit(solution)/shard_map/jit(_take)/gather | solution.py:37
  50.4 0.2 select_bitcast_fusion
  50.6 44.1 %all_to_all.18 = f32[8,2,32,768]{3,2,1,0:T(8,128)S(1)} all-to-all(f32[8,2,32,768]{3,2,1,0:T(8,128)S(1)} %select_bitcast_fusion), channel_id=1, replica_groups=mesh['grp'=4,'wide'=8] {'wide'}, dimensions={0} | all-to-all | bytes 3145728 | tf_op jit(solution)/shard_map/all_to_all | solution.py:41
  94.7 0.1 copy.28
  94.8 1.9 %all_to_all.16 = f32[2,256,3,256]{3,2,1,0:T(4,128)} reshape(f32[1,2,8,32,768]{4,3,2,1,0:T(8,128)S(1)} %copy.28) | data formatting | bytes 3145728 | tf_op jit(solution)/shard_map/all_to_all | solution.py:41
  96.7 1.8 %copy.29 = f32[2,256,3,256]{1,3,0,2:T(8,128)S(1)} copy(f32[2,256,3,256]{3,2,1,0:T(4,128)} %all_to_all.16) | data formatting | bytes 3145728 | tf_op jit(solution)/shard_map/all_to_all | solution.py:41
  98.5 0.2 bitcast_reduce_fusion
  98.7 10.1 %all-reduce = (f32[1,2,1,768]{3,1,2,0:T(2,128)S(1)}, f32[1,2,1,768]{3,1,2,0:T(2,128)S(1)}) all-reduce(f32[1,2,1,768]{3,1,2,0:T(2,128)S(1)} %bitcast.30, f32[1,2,1,768]{3,1,2,0:T(2,128)S(1)} %bitcast.29), channel_id=1, replica_groups=mesh['grp'=4,'wide'=8] {'grp'}, use_global_device_ids=true, to_apply=%region_3.4 | all-reduce | flops 3072 | bytes 24576 | tf_op jit(solution)/shard_map/psum | solution.py:42
  108.9 0.5 multiply_convert_fusion
  109.4 0.3 convolution_bitcast_fusion
  109.7 0.1 collective-permute-start
  109.8 2.6 %collective-permute-done = f32[2,2,256,256]{3,2,0,1:T(8,128)S(1)} collective-permute-done((f32[2,2,256,256]{3,2,0,1:T(8,128)S(1)}, f32[2,2,256,256]{3,2,0,1:T(8,128)S(1)}, u32[]{:S(2)}, u32[]{:S(2)}) %collective-permute-start) | collective-permute-done | bytes 1048608 | tf_op jit(solution)/shard_map/ppermute | solution.py:56
  112.4 0.1 add.86
  112.6 1.6 %collective-permute-start.1 = (f32[2,2,256,256]{3,2,0,1:T(8,128)S(1)}, f32[2,2,256,256]{3,2,0,1:T(8,128)S(1)}, u32[]{:S(2)}, u32[]{:S(2)}) collective-permute-start(f32[2,2,256,256]{3,2,0,1:T(8,128)S(1)} %add.86), channel_id=1, source_target_pairs={{0,16},{8,24},{16,0},{24,8},{1,17},{9,25},{17,1},{25,9},{2,18},{10... | collective-permute-start | bytes 3145736 | tf_op jit(solution)/shard_map/ppermute | solution.py:56
  114.2 23.7 %collective-permute-done.1 = f32[2,2,256,256]{3,2,0,1:T(8,128)S(1)} collective-permute-done((f32[2,2,256,256]{3,2,0,1:T(8,128)S(1)}, f32[2,2,256,256]{3,2,0,1:T(8,128)S(1)}, u32[]{:S(2)}, u32[]{:S(2)}) %collective-permute-start.1) | collective-permute-done | bytes 1048608 | tf_op jit(solution)/shard_map/ppermute | solution.py:56
  137.9 0.7 copy.31
  (7 shorter events, 0.1 us)
Async XLA Ops:
  109.7 2.7 %collective-permute-start = (f32[2,2,256,256]{3,2,0,1:T(8,128)S(1)}, f32[2,2,256,256]{3,2,0,1:T(8,128)S(1)}, u32[]{:S(2)}, u32[]{:S(2)}) collective-permute-start(f32[2,2,256,256]{3,2,0,1:T(8,128)S(1)} %convolution_bitcast_fusion), channel_id=1, source_target_pairs={{0,8},{8,0},{16,24},{24,16},{1,9},{9,1},{17,25},{25,17},{2,10},{10... | collective-permute-start | bytes 3145736 | tf_op jit(solution)/shard_map/ppermute | solution.py:56
  112.6 25.3 %collective-permute-start.1 = (f32[2,2,256,256]{3,2,0,1:T(8,128)S(1)}, f32[2,2,256,256]{3,2,0,1:T(8,128)S(1)}, u32[]{:S(2)}, u32[]{:S(2)}) collective-permute-start(f32[2,2,256,256]{3,2,0,1:T(8,128)S(1)} %add.86), channel_id=1, source_target_pairs={{0,16},{8,24},{16,0},{24,8},{1,17},{9,25},{17,1},{25,9},{2,18},{10... | collective-permute-start | bytes 3145736 | tf_op jit(solution)/shard_map/ppermute | solution.py:56
